TPU v7x, 256 devices: a whole 4x4x8 slice. The times are simulated.
256 devices in a mesh: shards: 16 (over x, y), tensor: 4 (over z_hi, core), replica: 4 (over z_lo).
Axes of the slice: x: 4, y: 4, z: 8 (z_hi: 2, z_lo: 4; z = z_hi * 4 + z_lo), core: 2. Of those that a mesh axis runs over, the one named last changes fastest.
Arguments:
- activations: bfloat16 [262144, 1024], P(('shards', 'tensor', 'replica')), may hold values from -24 to 24
- grads_out: bfloat16 [262144, 1024], P(('shards', 'tensor', 'replica')), may hold values from -24 to 24
- grad_parts: float32 [64, 1024, 1024], P(('shards', 'replica'), None, 'tensor'), may hold values from -80 to 80
- old_factors: float32 [16, 128, 128], replicated, may hold values from -16 to 16, as said below
- block_owner: int32 [16], replicated, may hold values from 0 to 15, as said below
- weights: float32 [1024, 1024], P(('shards', 'replica'), 'tensor'), may hold values from -0.1875 to 0.1875
- momentum: float32 [1024, 1024], P(('shards', 'replica'), 'tensor'), may hold values from -4 to 4
Outputs:
- weights_next: float32 [1024, 1024], P(None, 'tensor')
- momentum_next: float32 [1024, 1024], P(('shards', 'replica'), 'tensor')
- next_factor_blocks: float32 [32, 128, 128], P('shards')
Inputs may be any that keep to these rules, and one draw needn't show every extreme that they name: `block_owner`: each shard index owns at most 2 of the 16 blocks, and some index owns exactly 2. `old_factors`: each block is symmetric and positive definite.
All inputs are finite; a program needn't handle non-finite values. Where the computation divides by a largest or mean magnitude, that divisor is 1e-20 or more.
Results may differ from a plain program's by a relative error of at most 0.0003.
Values sent between devices are 32-bit elements; how exact they have to be, the bound alone decides.
No kernel may reach another device: no remote copies, remote signals or barrier semaphores. Data moves between devices by JAX's collectives and lax.ppermute only.
A program may use at most 64 MiB of HBM per device.

v0:
```python
import jax
import jax.numpy as jnp
from jax import lax
from jax.sharding import PartitionSpec as P

NS_STEPS = 4
exact_mode = lax.Precision.HIGHEST
decay_rate = 0.75
damping = 0.1
damp_shift = 0.001
clip_norm = 256.0
momentum_rate = 0.9
step_rate = 0.05


def sample_stats(samples, block_size):
    sample_rows, width = samples.shape
    blocks = samples.reshape(sample_rows, width // block_size, block_size)
    return jnp.einsum("tnb,tnc->nbc", blocks, blocks, preferred_element_type=jnp.float32)


def newton_inverse(mixed_factor_blocks):
    block_size = mixed_factor_blocks.shape[-1]
    identity = jnp.eye(block_size, dtype=jnp.float32)
    traces = jnp.trace(mixed_factor_blocks, axis1=1, axis2=2)
    damped = (
        mixed_factor_blocks + (damping * traces / block_size + damp_shift)[:, None, None] * identity
    )
    bounds = jnp.max(jnp.sum(jnp.abs(damped), axis=2), axis=1)
    approx = identity[None, :, :] / bounds[:, None, None]
    for iteration in range(NS_STEPS):
        left_part = jnp.einsum("nab,nbc->nac", approx, damped, precision=exact_mode)
        approx = 2.0 * approx - jnp.einsum("nab,nbc->nac", left_part, approx, precision=exact_mode)
    return approx


def swap(value, axis, flip):
    size = lax.axis_size(axis)
    return lax.ppermute(value, axis, [(i, i ^ flip) for i in range(size)])


def exchange_sum(value, axis):
    parts = [swap(value, axis, flip) for flip in range(1, lax.axis_size(axis))]
    for part in parts:
        value = value + part
    return value


def body(activations, grads_out, grad_parts, old_factors, block_owner, weights, momentum):
    shard_count = lax.axis_size("shards")
    block_count = old_factors.shape[0]
    block_size = old_factors.shape[1]
    capacity = (block_count + shard_count - 1) // shard_count + 1
    sample_count = (
        activations.shape[0] * shard_count * lax.axis_size("tensor") * lax.axis_size("replica")
    )
    partial_grad = grad_parts[0]
    row_count, col_count = partial_grad.shape
    left_count = row_count // block_size
    right_count = col_count // block_size
    base = weights - step_rate * momentum_rate * momentum
    base = lax.all_gather(base, "replica", axis=0, tiled=True)
    base = lax.all_gather(base, "shards", axis=0, tiled=True)
    stats = jnp.concatenate(
        [sample_stats(activations, block_size), sample_stats(grads_out, block_size)], axis=0
    )
    piece_rows = row_count // shard_count
    grad_pieces = [
        partial_grad[:, n * block_size : (n + 1) * block_size].reshape(
            shard_count, piece_rows, block_size
        )
        for n in range(right_count)
    ]
    outgoing = jnp.concatenate([stats] + grad_pieces, axis=1)
    incoming = lax.all_to_all(outgoing, "shards", 0, 0)
    summed = exchange_sum(jnp.sum(incoming, axis=0), "replica")
    own_stats = summed[:block_size]
    own_stats = own_stats + swap(own_stats, "tensor", 1)
    own_stats = own_stats + swap(own_stats, "tensor", 2)
    own = jnp.concatenate([own_stats, summed[block_size:]], axis=0)
    own, base = lax.optimization_barrier((own, base))
    gathered = lax.all_to_all(
        jnp.broadcast_to(own[None], (shard_count,) + own.shape), "shards", 0, 0
    )
    blended = decay_rate * old_factors + (1.0 - decay_rate) * (
        gathered[:, :block_size] / sample_count
    )
    grad_columns = [
        gathered[:, block_size + n * piece_rows : block_size + (n + 1) * piece_rows].reshape(
            left_count, block_size, block_size
        )
        for n in range(right_count)
    ]
    positions = jnp.arange(block_count, dtype=jnp.int32)
    earlier = (block_owner[:, None] == block_owner[None, :]) & (
        positions[None, :] < positions[:, None]
    )
    slots = block_owner * capacity + jnp.sum(earlier.astype(jnp.int32), axis=1)
    owned = []
    for place in range(capacity):
        match = slots == lax.axis_index("shards") * capacity + place
        which = jnp.sum(jnp.where(match, positions, 0))
        block = lax.dynamic_index_in_dim(blended, which, 0, keepdims=False)
        owned.append(jnp.where(jnp.any(match), block, 0.0))
    owned_blocks = jnp.stack(owned)
    right_first = left_count + lax.axis_index("tensor") * right_count
    needed = jnp.concatenate(
        [blended[:left_count], lax.dynamic_slice_in_dim(blended, right_first, right_count, 0)],
        axis=0,
    )
    inverses = newton_inverse(needed)
    precond_columns = []
    for n in range(right_count):
        left_part = jnp.einsum(
            "nab,nbc->nac", inverses[:left_count], grad_columns[n], precision=exact_mode
        )
        precond_columns.append(
            jnp.einsum("nab,bc->nac", left_part, inverses[left_count + n], precision=exact_mode)
        )
    local_sum = sum((jnp.sum(p * g) for p, g in zip(precond_columns, grad_columns)))
    precond = jnp.concatenate([p.reshape(row_count, block_size) for p in precond_columns], axis=1)
    alignment_sum = lax.psum(local_sum, "tensor")
    clip_scale = jnp.minimum(1.0, clip_norm / jnp.sqrt(alignment_sum))
    own_rows = weights.shape[0]
    first_row = lax.axis_index(("shards", "replica")) * own_rows
    own_precond = lax.dynamic_slice_in_dim(precond, first_row, own_rows, 0)
    momentum_next = momentum_rate * momentum + clip_scale * own_precond
    weights_next = base - step_rate * clip_scale * precond
    return (weights_next, momentum_next, owned_blocks)


def solution(mesh):
    placed = (
        P(("shards", "tensor", "replica"), None),
        P(("shards", "tensor", "replica"), None),
        P(("shards", "replica"), None, "tensor"),
        P(),
        P(),
        P(("shards", "replica"), "tensor"),
        P(("shards", "replica"), "tensor"),
    )
    return jax.shard_map(
        body,
        mesh=mesh,
        in_specs=placed,
        out_specs=(P(None, "tensor"), P(("shards", "replica"), "tensor"), P("shards", None, None)),
        check_vma=False,
    )
```

profile of v0, /device:TPU:1, one launch (start us, length us, event | category | flops | bytes accessed | tf_op | source)
XLA Modules:
  0.0 160.7 jit_solution(14424945549130774064)
XLA Ops:
  7.2 0.0 copy-start
  7.2 0.0 copy-start.7
  7.2 1.6 copy-done
  8.8 1.1 fusion.3
  9.8 0.0 copy-done.7
  9.8 0.0 copy-start.3
  9.8 1.1 fusion
  11.0 0.1 copy-done.3
  11.1 0.1 fusion.27
  11.1 1.5 pad_maximum_fusion
  12.6 0.0 copy-start.4
  12.6 0.0 copy-start.5
  12.6 7.8 %all-to-all-start = ((f32[16,256,128]{2,1,0:T(8,128)}), f32[16,256,128]{2,1,0:T(8,128)}, u32[]{:S(2)}, u32[]{:S(2)}) async-start(f32[16,256,128]{2,1,0:T(8,128)} %pad_maximum_fusion), calls=%async_computation | async-start | bytes 4194304 | tf_op jit(solution)/shard_map/all_to_all | solution.py:75
  20.4 0.0 all-gather.2.cloned.1.call-start
  20.4 0.0 copy-done.4
  20.4 0.0 copy-done.5
  20.5 13.0 %all_gather.6 = f32[64,256]{1,0:T(8,128)} all-gather(f32[16,256]{1,0:T(8,128)S(1)} %multiply_subtract_fusion), channel_id=1, replica_groups=mesh['shards'=16,'tensor'=4,'replica'=4] {'replica'}, dimensions={0}, use_global_device_ids=true | all-gather | bytes 81920 | tf_op jit(solution)/shard_map/all_gather | solution.py:62
  33.4 0.0 all-gather.2.cloned.1.call-update
  33.4 14.8 %all-to-all-done = f32[16,256,128]{2,1,0:T(8,128)} async-done(((f32[16,256,128]{2,1,0:T(8,128)}), f32[16,256,128]{2,1,0:T(8,128)}, u32[]{:S(2)}, u32[]{:S(2)}) %all-to-all-start) | async-done | bytes 2097184 | tf_op jit(solution)/shard_map/all_to_all | solution.py:75
  48.3 1.7 %reduce_sum.73 = f32[256,128]{1,0:T(8,128)S(1)} reduce(f32[16,256,128]{2,1,0:T(8,128)} %all-to-all-done, f32[]{:T(128)} %constant.25.clone.1), dimensions={0}, to_apply=%region_0.0 | reduce | flops 491520 | bytes 2228228 | tf_op jit(solution)/shard_map/reduce_sum | solution.py:76
  50.0 4.5 %collective-permute-start.2 = (f32[256,128]{1,0:T(8,128)S(1)}, f32[256,128]{1,0:T(8,128)S(1)}, u32[]{:S(2)}, u32[]{:S(2)}) collective-permute-start(f32[256,128]{1,0:T(8,128)S(1)} %reduce_sum.73), channel_id=1, source_target_pairs={{0,3},{1,2},{2,1},{3,0},{4,7},{5,6},{6,5},{7,4},{8,11},{9,10},{10,... | collective-permute-start | bytes 393224 | tf_op jit(solution)/shard_map/ppermute | solution.py:39
  54.5 0.0 collective-permute-start.1
  54.5 0.4 collective-permute-start
  54.8 2.0 %collective-permute-done.2 = f32[256,128]{1,0:T(8,128)S(1)} collective-permute-done((f32[256,128]{1,0:T(8,128)S(1)}, f32[256,128]{1,0:T(8,128)S(1)}, u32[]{:S(2)}, u32[]{:S(2)}) %collective-permute-start.2) | collective-permute-done | bytes 131104 | tf_op jit(solution)/shard_map/ppermute | solution.py:39
  56.9 7.0 %collective-permute-done.1 = f32[256,128]{1,0:T(8,128)S(1)} collective-permute-done((f32[256,128]{1,0:T(8,128)S(1)}, f32[256,128]{1,0:T(8,128)S(1)}, u32[]{:S(2)}, u32[]{:S(2)}) %collective-permute-start.1) | collective-permute-done | bytes 131104 | tf_op jit(solution)/shard_map/ppermute | solution.py:39
  63.9 0.0 collective-permute-done
  64.0 2.2 %collective-permute-start.3 = (f32[128,128]{1,0:T(8,128)S(1)}, f32[128,128]{1,0:T(8,128)S(1)}, u32[]{:S(2)}, u32[]{:S(2)}) collective-permute-start(f32[128,128]{1,0:T(8,128)S(1)} %slice.47), channel_id=1, source_target_pairs={{0,4},{4,0},{8,12},{12,8},{1,5},{5,1},{9,13},{13,9},{2,6},{6,2},{1... | collective-permute-start | bytes 196616 | tf_op jit(solution)/shard_map/ppermute | solution.py:39
  66.1 0.9 collective-permute-done.3
  67.1 5.9 %collective-permute-start.4 = (f32[128,128]{1,0:T(8,128)S(1)}, f32[128,128]{1,0:T(8,128)S(1)}, u32[]{:S(2)}, u32[]{:S(2)}) collective-permute-start(f32[128,128]{1,0:T(8,128)S(1)} %get-tuple-element.18), channel_id=1, source_target_pairs={{0,8},{4,12},{8,0},{12,4},{1,9},{5,13},{9,1},{13,5},{2,10},{6,14},... | collective-permute-start | bytes 196616 | tf_op jit(solution)/shard_map/ppermute | solution.py:39
  73.0 2.2 %collective-permute-done.4 = f32[128,128]{1,0:T(8,128)S(1)} collective-permute-done((f32[128,128]{1,0:T(8,128)S(1)}, f32[128,128]{1,0:T(8,128)S(1)}, u32[]{:S(2)}, u32[]{:S(2)}) %collective-permute-start.4) | collective-permute-done | bytes 65568 | tf_op jit(solution)/shard_map/ppermute | solution.py:39
  75.2 9.0 %all-gather.2.cloned.1.call-done = f32[1024,256]{1,0:T(8,128)} async-done(((f32[64,256]{1,0:T(8,128)}), f32[1024,256]{1,0:T(8,128)}) %all-gather.2.cloned.1.call-update) | async-done | bytes 1048592 | tf_op jit(solution)/shard_map/all_gather | solution.py:63
  84.2 1.5 broadcast_in_dim.33
  85.7 5.2 %all-to-all-start.1 = ((f32[16,256,128]{2,1,0:T(8,128)}), f32[16,256,128]{2,1,0:T(8,128)}, u32[]{:S(2)}, u32[]{:S(2)}) async-start(f32[16,256,128]{2,1,0:T(8,128)} %broadcast_in_dim.33), calls=%async_computation.1 | async-start | bytes 4194304 | tf_op jit(solution)/shard_map/all_to_all | solution.py:82
  90.9 0.0 copy-done.6
  90.9 0.2 convert_reduce_fusion
  91.0 0.7 compare_reduce_fusion.1
  91.8 0.7 fusion.21
  95.8 20.6 %all-to-all-done.1 = f32[16,256,128]{2,1,0:T(8,128)} async-done(((f32[16,256,128]{2,1,0:T(8,128)}), f32[16,256,128]{2,1,0:T(8,128)}, u32[]{:S(2)}, u32[]{:S(2)}) %all-to-all-start.1) | async-done | bytes 2097184 | tf_op jit(solution)/shard_map/all_to_all | solution.py:82
  116.5 0.0 copy-done.2
  116.5 1.4 fusion.8
  117.8 0.0 copy-start.1
  117.9 0.9 copy-done.1
  118.8 0.2 select_reduce_fusion
  119.0 0.3 abs_reduce_fusion
  119.3 0.1 reduce_max.9
  119.4 0.9 fusion.9
  120.3 0.8 convolution_subtract_fusion.3
  121.2 0.8 fusion.25
  122.0 0.8 convolution_subtract_fusion.2
  122.8 0.8 fusion.24
  123.6 0.8 convolution_subtract_fusion.1
  124.4 0.8 fusion.23
  125.3 0.8 convolution_subtract_fusion
  126.1 1.3 fusion.26
  127.4 0.6 fusion.28
  128.0 0.6 fusion.17
  128.6 0.6 fusion.29
  129.3 0.6 fusion.16
  129.9 0.8 multiply_reduce_fusion
  132.7 14.8 %psum.7 = f32[]{:T(128)} all-reduce(f32[]{:T(128)S(6)} %add.69), channel_id=1, replica_groups=mesh['shards'=16,'tensor'=4,'replica'=4] {'tensor'}, use_global_device_ids=true, to_apply=%region_6.7 | all-reduce | flops 1 | bytes 8 | tf_op jit(solution)/shard_map/psum | solution.py:122
  148.1 2.1 %dynamic-slice_select_fusion.1 = (f32[1,128,128]{2,1,0:T(8,128)S(1)}, f32[1,128,128]{2,1,0:T(8,128)S(1)}) fusion(f32[16,128,128]{2,1,0:T(8,128)} %copy-done.1, s32[]{:T(128)S(6)} %select_n.46, pred[]{:T(512)} %get-tuple-element.7, s32[]{:T(128)S(6)} %select_n.50, pred[]{:T(512)} %get-tuple-element.8), kind=kLoop, calls=%fused_computation.39 | loop fusion | flops 32768 | bytes 262154 | tf_op jit(solution)/shard_map/jit(_where)/select_n | solution.py:104
  150.3 0.7 pad_maximum_fusion.4
  151.0 0.6 multiply_add_fusion.1
  151.6 2.3 %fusion.7 = f32[1024,256]{1,0:T(8,128)} fusion(f32[1024,256]{1,0:T(8,128)} %all-gather.2.cloned.1.call-done, f32[1024,128]{1,0:T(8,128)S(1)} %bitcast.51, f32[1024,128]{1,0:T(8,128)S(1)} %bitcast.49, f32[]{:T(128)S(6)} %mul_shard_map.3), kind=kLoop, calls=%fused_computation.15 | loop fusion | flops 786432 | bytes 3145732 | tf_op jit(solution)/shard_map/sub | solution.py:128
  (13 shorter events, 0.2 us)
Async XLA Ops:
  7.2 1.6 copy-start
  7.2 2.6 %copy-start.7 = (bf16[1024,1024]{1,0:T(8,128)(2,1)S(1)}, bf16[1024,1024]{1,0:T(8,128)(2,1)}, u32[]{:S(2)}) copy-start(bf16[1024,1024]{1,0:T(8,128)(2,1)} %param.8) | copy-start | bytes 6291460
  9.8 1.2 copy-start.3
  12.6 7.8 %copy-start.4 = (f32[16,256]{1,0:T(8,128)S(1)}, f32[16,256]{1,0:T(8,128)}, u32[]{:S(2)}) copy-start(f32[16,256]{1,0:T(8,128)} %param.13) | copy-start | bytes 49156
  12.6 7.8 %copy-start.5 = (f32[16,256]{1,0:T(8,128)S(1)}, f32[16,256]{1,0:T(8,128)}, u32[]{:S(2)}) copy-start(f32[16,256]{1,0:T(8,128)} %param.12) | copy-start | bytes 49156
  12.6 35.7 %all-to-all-start = ((f32[16,256,128]{2,1,0:T(8,128)}), f32[16,256,128]{2,1,0:T(8,128)}, u32[]{:S(2)}, u32[]{:S(2)}) async-start(f32[16,256,128]{2,1,0:T(8,128)} %pad_maximum_fusion), calls=%async_computation | async-start | bytes 4194304 | tf_op jit(solution)/shard_map/all_to_all | solution.py:75
  20.4 63.8 %all-gather.2.cloned.1.call-start = ((), (), s32[]{:S(2)}) async-start(), calls=%async_computation.2 | async-start | bytes 1114112 | tf_op jit(solution)/shard_map/all_gather | solution.py:63
  50.0 6.9 %collective-permute-start.2 = (f32[256,128]{1,0:T(8,128)S(1)}, f32[256,128]{1,0:T(8,128)S(1)}, u32[]{:S(2)}, u32[]{:S(2)}) collective-permute-start(f32[256,128]{1,0:T(8,128)S(1)} %reduce_sum.73), channel_id=1, source_target_pairs={{0,3},{1,2},{2,1},{3,0},{4,7},{5,6},{6,5},{7,4},{8,11},{9,10},{10,... | collective-permute-start | bytes 393224 | tf_op jit(solution)/shard_map/ppermute | solution.py:39
  54.5 9.4 %collective-permute-start.1 = (f32[256,128]{1,0:T(8,128)S(1)}, f32[256,128]{1,0:T(8,128)S(1)}, u32[]{:S(2)}, u32[]{:S(2)}) collective-permute-start(f32[256,128]{1,0:T(8,128)S(1)} %reduce_sum.73), channel_id=1, source_target_pairs={{0,2},{1,3},{2,0},{3,1},{4,6},{5,7},{6,4},{7,5},{8,10},{9,11},{10,... | collective-permute-start | bytes 393224 | tf_op jit(solution)/shard_map/ppermute | solution.py:39
  54.5 9.4 %collective-permute-start = (f32[256,128]{1,0:T(8,128)S(1)}, f32[256,128]{1,0:T(8,128)S(1)}, u32[]{:S(2)}, u32[]{:S(2)}) collective-permute-start(f32[256,128]{1,0:T(8,128)S(1)} %reduce_sum.73), channel_id=1, source_target_pairs={{0,1},{1,0},{2,3},{3,2},{4,5},{5,4},{6,7},{7,6},{8,9},{9,8},{10,11... | collective-permute-start | bytes 393224 | tf_op jit(solution)/shard_map/ppermute | solution.py:39
  64.0 3.1 %collective-permute-start.3 = (f32[128,128]{1,0:T(8,128)S(1)}, f32[128,128]{1,0:T(8,128)S(1)}, u32[]{:S(2)}, u32[]{:S(2)}) collective-permute-start(f32[128,128]{1,0:T(8,128)S(1)} %slice.47), channel_id=1, source_target_pairs={{0,4},{4,0},{8,12},{12,8},{1,5},{5,1},{9,13},{13,9},{2,6},{6,2},{1... | collective-permute-start | bytes 196616 | tf_op jit(solution)/shard_map/ppermute | solution.py:39
  67.1 8.1 %collective-permute-start.4 = (f32[128,128]{1,0:T(8,128)S(1)}, f32[128,128]{1,0:T(8,128)S(1)}, u32[]{:S(2)}, u32[]{:S(2)}) collective-permute-start(f32[128,128]{1,0:T(8,128)S(1)} %get-tuple-element.18), channel_id=1, source_target_pairs={{0,8},{4,12},{8,0},{12,4},{1,9},{5,13},{9,1},{13,5},{2,10},{6,14},... | collective-permute-start | bytes 196616 | tf_op jit(solution)/shard_map/ppermute | solution.py:39
  85.7 5.2 %copy-start.6 = (s32[16]{0:T(128)S(1)}, s32[16]{0:T(128)}, u32[]{:S(2)}) copy-start(s32[16]{0:T(128)} %param.11) | copy-start | bytes 196
  85.7 30.8 %copy-start.2 = (f32[16,128,128]{2,1,0:T(8,128)S(1)}, f32[16,128,128]{2,1,0:T(8,128)}, u32[]{:S(2)}) copy-start(f32[16,128,128]{2,1,0:T(8,128)} %param.10) | copy-start | bytes 3145732
  85.7 30.8 %all-to-all-start.1 = ((f32[16,256,128]{2,1,0:T(8,128)}), f32[16,256,128]{2,1,0:T(8,128)}, u32[]{:S(2)}, u32[]{:S(2)}) async-start(f32[16,256,128]{2,1,0:T(8,128)} %broadcast_in_dim.33), calls=%async_computation.1 | async-start | bytes 4194304 | tf_op jit(solution)/shard_map/all_to_all | solution.py:82
  117.8 1.0 copy-start.1
Sparse Core Ops, SparseCore 0:
  33.6 50.5 all-gather.1
where the time goes:
time: 161 us
  waiting for transfers between devices  56.6 us (35%)
  blocking collectives  27.7 us (17%)
  starting transfers between devices  25.9 us (16%)
  between operations  20.3 us (13%)
  other arithmetic  13.4 us (8%)
  matrix products  11.2 us (7%)
  local copies, waits for them, and re-layouts  5.53 us (3%)
    all_to_all x1, waiting for transfers between devices, body(): lax.all_to_all(jnp.broadcast_to(own[None], (shard_count,) + own.shape), '...  20.6 us
    all_to_all x1, waiting for transfers between devices, body(): incoming = lax.all_to_all(outgoing, 'shards', 0, 0)  14.8 us
    psum x1, blocking collectives, body(): alignment_sum = lax.psum(local_sum, 'tensor')  14.8 us
    ppermute x5, starting transfers between devices, swap(): return lax.ppermute(value, axis, [(i, i ^ flip) for i in range(size)])  13 us
    all_gather x1, blocking collectives, body(): base = lax.all_gather(base, 'replica', axis=0, tiled=True)  13 us
    ppermute x5, waiting for transfers between devices, swap(): return lax.ppermute(value, axis, [(i, i ^ flip) for i in range(size)])  12.1 us
    all_gather x1, waiting for transfers between devices, body(): base = lax.all_gather(base, 'shards', axis=0, tiled=True)  8.98 us
    all_to_all x1, starting transfers between devices, body(): incoming = lax.all_to_all(outgoing, 'shards', 0, 0)  7.77 us
  transfers between devices with their start and end apart: 8, of which 7 were waited for; matrix products, arithmetic and copies ran while one was open for 2% of the time, Pallas kernels for 0%

commit v1 on v0

--- a/solution.py
+++ b/solution.py
@@ -60,7 +60,9 @@
     right_count = col_count // block_size
     base = weights - step_rate * momentum_rate * momentum
     base = lax.all_gather(base, "replica", axis=0, tiled=True)
-    base = lax.all_gather(base, "shards", axis=0, tiled=True)
+    extra = jnp.stack([base] * lax.axis_size("shards"), 0)
+    view_out = lax.all_to_all(extra, "shards", 0, 0)
+    base = jnp.concatenate(view_out, 0)
     stats = jnp.concatenate(
         [sample_stats(activations, block_size), sample_stats(grads_out, block_size)], axis=0
     )

time: 161 us -> 146 us (0.907)
  between operations: 20.3 us -> 6.95 us
  waiting for transfers between devices: 56.6 us -> 49.3 us
  starting transfers between devices: 25.9 us -> 31.2 us
    all_gather x1 -> x0, waiting for transfers between devices: 8.98 us -> none  [body(): base = lax.all_gather(base, 'shards', axis=0, tiled=True)]
    all_to_all x0 -> x1, starting transfers between devices: none -> 3.91 us  [body(): view_out = lax.all_to_all(extra, 'shards', 0, 0)]
    all_to_all x1, starting transfers between devices: 5.17 us -> 6.89 us  [body(): lax.all_to_all(jnp.broadcast_to(own[None], (shard_count,) + own.shape), '...]
  transfers between devices with their start and end apart: 8 -> 8, of which waited for: 7 -> 6; matrix products, arithmetic and copies ran while one was open for 2% -> 2% of each run, Pallas kernels for 0% -> 0%
where the time goes in v1:
time: 146 us
  waiting for transfers between devices  49.3 us (34%)
  starting transfers between devices  31.2 us (21%)
  blocking collectives  26.7 us (18%)
  other arithmetic  13.6 us (9%)
  matrix products  11.2 us (8%)
  between operations  6.95 us (5%)
  local copies, waits for them, and re-layouts  6.74 us (5%)
    all_to_all x1, waiting for transfers between devices, body(): lax.all_to_all(jnp.broadcast_to(own[None], (shard_count,) + own.shape), '...  21.6 us
    all_to_all x1, waiting for transfers between devices, body(): incoming = lax.all_to_all(outgoing, 'shards', 0, 0)  15.2 us
    psum x1, blocking collectives, body(): alignment_sum = lax.psum(local_sum, 'tensor')  14.1 us
    all_gather x1, blocking collectives, body(): base = lax.all_gather(base, 'replica', axis=0, tiled=True)  12.7 us
    ppermute x5, starting transfers between devices, swap(): return lax.ppermute(value, axis, [(i, i ^ flip) for i in range(size)])  12.6 us
    ppermute x5, waiting for transfers between devices, swap(): return lax.ppermute(value, axis, [(i, i ^ flip) for i in range(size)])  12.4 us
    all_to_all x1, starting transfers between devices, body(): incoming = lax.all_to_all(outgoing, 'shards', 0, 0)  7.77 us
    all_to_all x1, starting transfers between devices, body(): lax.all_to_all(jnp.broadcast_to(own[None], (shard_count,) + own.shape), '...  6.89 us
  transfers between devices with their start and end apart: 8, of which 6 were waited for; matrix products, arithmetic and copies ran while one was open for 2% of the time, Pallas kernels for 0%

profile of v1, /device:TPU:1, one launch (start us, length us, event | category | flops | bytes accessed | tf_op | source)
XLA Modules:
  0.0 145.7 jit_solution(14053450389647477167)
XLA Ops:
  0.6 0.0 copy-start
  0.6 0.0 copy-start.7
  0.7 1.6 %copy-done = bf16[1024,1024]{1,0:T(8,128)(2,1)S(1)} copy-done((bf16[1024,1024]{1,0:T(8,128)(2,1)S(1)}, bf16[1024,1024]{1,0:T(8,128)(2,1)}, u32[]{:S(2)}) %copy-start) | copy-done | bytes 2097176
  2.2 1.1 fusion.3
  3.3 0.0 copy-done.7
  3.3 0.0 copy-start.3
  3.3 1.1 fusion
  4.5 0.1 copy-done.3
  4.5 0.1 fusion.27
  4.6 1.5 %pad_maximum_fusion = f32[16,256,128]{2,1,0:T(8,128)} fusion(f32[16,64,128]{2,1,0:T(8,128)S(1)} %bitcast.59, f32[16,64,128]{2,1,0:T(8,128)S(1)} %bitcast.58, f32[8,128,128]{2,1,0:T(8,128)S(1)} %fusion, f32[8,128,128]{2,1,0:T(8,128)S(1)} %fusion.3), kind=kLoop, calls=%fused_computation.6 | loop fusion | flops 1572864 | bytes 4194304 | tf_op jit(solution)/shard_map/concatenate | solution.py:76
  6.1 0.0 copy-start.4
  6.1 7.8 %all-to-all-start = ((f32[16,256,128]{2,1,0:T(8,128)}), f32[16,256,128]{2,1,0:T(8,128)}, u32[]{:S(2)}, u32[]{:S(2)}) async-start(f32[16,256,128]{2,1,0:T(8,128)} %pad_maximum_fusion), calls=%async_computation | async-start | bytes 4194304 | tf_op jit(solution)/shard_map/all_to_all | solution.py:77
  13.8 0.0 copy-done.4
  13.8 0.0 copy-done.5
  13.9 12.7 %all_gather.3 = f32[64,256]{1,0:T(8,128)S(1)} all-gather(f32[16,256]{1,0:T(8,128)S(1)} %multiply_subtract_fusion), channel_id=1, replica_groups=mesh['shards'=16,'tensor'=4,'replica'=4] {'replica'}, dimensions={0}, use_global_device_ids=true | all-gather | bytes 81920 | tf_op jit(solution)/shard_map/all_gather | solution.py:62
  26.5 15.2 %all-to-all-done = f32[16,256,128]{2,1,0:T(8,128)} async-done(((f32[16,256,128]{2,1,0:T(8,128)}), f32[16,256,128]{2,1,0:T(8,128)}, u32[]{:S(2)}, u32[]{:S(2)}) %all-to-all-start) | async-done | bytes 2097184 | tf_op jit(solution)/shard_map/all_to_all | solution.py:77
  41.8 1.1 stack.4
  42.8 3.9 %all-to-all-start.1 = ((f32[16,64,256]{2,1,0:T(8,128)}), f32[16,64,256]{2,1,0:T(8,128)S(1)}, u32[]{:S(2)}, u32[]{:S(2)}) async-start(f32[16,64,256]{2,1,0:T(8,128)} %stack.4), calls=%async_computation.1 | async-start | bytes 2097152 | tf_op jit(solution)/shard_map/all_to_all | solution.py:64
  46.8 1.7 %reduce_sum.73 = f32[256,128]{1,0:T(8,128)S(1)} reduce(f32[16,256,128]{2,1,0:T(8,128)} %all-to-all-done, f32[]{:T(128)} %constant.25.clone.1), dimensions={0}, to_apply=%region_0.0 | reduce | flops 491520 | bytes 2228228 | tf_op jit(solution)/shard_map/reduce_sum | solution.py:78
  48.5 4.4 %collective-permute-start.2 = (f32[256,128]{1,0:T(8,128)S(1)}, f32[256,128]{1,0:T(8,128)S(1)}, u32[]{:S(2)}, u32[]{:S(2)}) collective-permute-start(f32[256,128]{1,0:T(8,128)S(1)} %reduce_sum.73), channel_id=1, source_target_pairs={{0,3},{1,2},{2,1},{3,0},{4,7},{5,6},{6,5},{7,4},{8,11},{9,10},{10,... | collective-permute-start | bytes 393224 | tf_op jit(solution)/shard_map/ppermute | solution.py:39
  52.9 0.0 collective-permute-start.1
  52.9 0.4 collective-permute-start
  53.3 2.3 %collective-permute-done.2 = f32[256,128]{1,0:T(8,128)S(1)} collective-permute-done((f32[256,128]{1,0:T(8,128)S(1)}, f32[256,128]{1,0:T(8,128)S(1)}, u32[]{:S(2)}, u32[]{:S(2)}) %collective-permute-start.2) | collective-permute-done | bytes 131104 | tf_op jit(solution)/shard_map/ppermute | solution.py:39
  55.6 7.1 %collective-permute-done.1 = f32[256,128]{1,0:T(8,128)S(1)} collective-permute-done((f32[256,128]{1,0:T(8,128)S(1)}, f32[256,128]{1,0:T(8,128)S(1)}, u32[]{:S(2)}, u32[]{:S(2)}) %collective-permute-start.1) | collective-permute-done | bytes 131104 | tf_op jit(solution)/shard_map/ppermute | solution.py:39
  62.6 0.0 collective-permute-done
  62.7 1.9 %collective-permute-start.3 = (f32[128,128]{1,0:T(8,128)S(1)}, f32[128,128]{1,0:T(8,128)S(1)}, u32[]{:S(2)}, u32[]{:S(2)}) collective-permute-start(f32[128,128]{1,0:T(8,128)S(1)} %slice.47), channel_id=1, source_target_pairs={{0,4},{4,0},{8,12},{12,8},{1,5},{5,1},{9,13},{13,9},{2,6},{6,2},{1... | collective-permute-start | bytes 196616 | tf_op jit(solution)/shard_map/ppermute | solution.py:39
  64.6 0.9 collective-permute-done.3
  65.5 5.9 %collective-permute-start.4 = (f32[128,128]{1,0:T(8,128)S(1)}, f32[128,128]{1,0:T(8,128)S(1)}, u32[]{:S(2)}, u32[]{:S(2)}) collective-permute-start(f32[128,128]{1,0:T(8,128)S(1)} %get-tuple-element.18), channel_id=1, source_target_pairs={{0,8},{4,12},{8,0},{12,4},{1,9},{5,13},{9,1},{13,5},{2,10},{6,14},... | collective-permute-start | bytes 196616 | tf_op jit(solution)/shard_map/ppermute | solution.py:39
  71.4 2.2 %collective-permute-done.4 = f32[128,128]{1,0:T(8,128)S(1)} collective-permute-done((f32[128,128]{1,0:T(8,128)S(1)}, f32[128,128]{1,0:T(8,128)S(1)}, u32[]{:S(2)}, u32[]{:S(2)}) %collective-permute-start.4) | collective-permute-done | bytes 65568 | tf_op jit(solution)/shard_map/ppermute | solution.py:39
  73.6 0.0 all-to-all-done.1
  73.6 0.0 copy-start.1
  73.6 1.6 %broadcast_in_dim.33 = f32[16,256,128]{2,1,0:T(8,128)} broadcast(f32[256,128]{1,0:T(8,128)S(1)} %pad_maximum_fusion.3), dimensions={1,2} | broadcast | bytes 2228224 | tf_op jit(solution)/shard_map/broadcast_in_dim | solution.py:85
  75.3 0.0 copy-done.1
  75.3 6.9 %all-to-all-start.2 = ((f32[16,256,128]{2,1,0:T(8,128)}), f32[16,256,128]{2,1,0:T(8,128)}, u32[]{:S(2)}, u32[]{:S(2)}) async-start(f32[16,256,128]{2,1,0:T(8,128)} %broadcast_in_dim.33), calls=%async_computation.2 | async-start | bytes 4194304 | tf_op jit(solution)/shard_map/all_to_all | solution.py:84
  82.2 0.0 copy-done.6
  82.2 0.2 convert_reduce_fusion
  82.4 0.7 compare_reduce_fusion.1
  83.1 0.7 fusion.21
  87.1 21.6 %all-to-all-done.2 = f32[16,256,128]{2,1,0:T(8,128)} async-done(((f32[16,256,128]{2,1,0:T(8,128)}), f32[16,256,128]{2,1,0:T(8,128)}, u32[]{:S(2)}, u32[]{:S(2)}) %all-to-all-start.2) | async-done | bytes 2097184 | tf_op jit(solution)/shard_map/all_to_all | solution.py:84
  108.7 1.7 %fusion.8 = f32[16,128,128]{2,1,0:T(8,128)S(1)} fusion(f32[16,256,128]{2,1,0:T(8,128)} %all-to-all-done.2, f32[16,128,128]{2,1,0:T(8,128)} %param.10), kind=kLoop, calls=%fused_computation.17 | loop fusion | flops 786432 | bytes 3145728 | tf_op jit(solution)/shard_map/add | solution.py:87
  110.4 0.0 copy-start.2
  110.4 0.9 copy-done.2
  111.4 0.2 select_reduce_fusion
  111.6 0.3 abs_reduce_fusion
  111.9 0.1 reduce_max.9
  112.0 0.9 fusion.9
  112.9 0.8 convolution_subtract_fusion.3
  113.7 0.8 fusion.25
  114.6 0.8 convolution_subtract_fusion.2
  115.4 0.8 fusion.24
  116.2 0.8 convolution_subtract_fusion.1
  117.0 0.8 fusion.23
  117.8 0.8 convolution_subtract_fusion
  118.6 1.3 fusion.26
  120.0 0.6 fusion.28
  120.6 0.6 fusion.17
  121.2 0.6 fusion.29
  121.8 0.6 fusion.16
  122.4 0.8 multiply_reduce_fusion
  125.2 14.1 %psum.7 = f32[]{:T(128)} all-reduce(f32[]{:T(128)S(6)} %add.69), channel_id=1, replica_groups=mesh['shards'=16,'tensor'=4,'replica'=4] {'tensor'}, use_global_device_ids=true, to_apply=%region_6.7 | all-reduce | flops 1 | bytes 8 | tf_op jit(solution)/shard_map/psum | solution.py:124
  140.0 2.1 %dynamic-slice_select_fusion.1 = (f32[1,128,128]{2,1,0:T(8,128)S(1)}, f32[1,128,128]{2,1,0:T(8,128)S(1)}) fusion(f32[16,128,128]{2,1,0:T(8,128)} %copy-done.2, s32[]{:T(128)S(6)} %select_n.46, pred[]{:T(512)} %get-tuple-element.7, s32[]{:T(128)S(6)} %select_n.50, pred[]{:T(512)} %get-tuple-element.8), kind=kLoop, calls=%fused_computation.39 | loop fusion | flops 32768 | bytes 262154 | tf_op jit(solution)/shard_map/jit(_where)/select_n | solution.py:106
  142.1 0.7 pad_maximum_fusion.4
  142.8 0.6 multiply_add_fusion.1
  143.4 2.3 %fusion.7 = f32[1024,256]{1,0:T(8,128)} fusion(f32[1024,256]{1,0:T(8,128)} %bitcast.53, f32[1024,128]{1,0:T(8,128)S(1)} %bitcast.52, f32[1024,128]{1,0:T(8,128)S(1)} %bitcast.50, f32[]{:T(128)S(6)} %mul_shard_map.3), kind=kLoop, calls=%fused_computation.15 | loop fusion | flops 786432 | bytes 3145732 | tf_op jit(solution)/shard_map/sub | solution.py:130
  (13 shorter events, 0.2 us)
Async XLA Ops:
  0.6 1.6 %copy-start = (bf16[1024,1024]{1,0:T(8,128)(2,1)S(1)}, bf16[1024,1024]{1,0:T(8,128)(2,1)}, u32[]{:S(2)}) copy-start(bf16[1024,1024]{1,0:T(8,128)(2,1)} %param.7) | copy-start | bytes 6291460
  0.6 2.6 %copy-start.7 = (bf16[1024,1024]{1,0:T(8,128)(2,1)S(1)}, bf16[1024,1024]{1,0:T(8,128)(2,1)}, u32[]{:S(2)}) copy-start(bf16[1024,1024]{1,0:T(8,128)(2,1)} %param.8) | copy-start | bytes 6291460
  3.3 1.2 copy-start.3
  6.1 7.8 %copy-start.4 = (f32[16,256]{1,0:T(8,128)S(1)}, f32[16,256]{1,0:T(8,128)}, u32[]{:S(2)}) copy-start(f32[16,256]{1,0:T(8,128)} %param.13) | copy-start | bytes 49156
  6.1 7.8 %copy-start.5 = (f32[16,256]{1,0:T(8,128)S(1)}, f32[16,256]{1,0:T(8,128)}, u32[]{:S(2)}) copy-start(f32[16,256]{1,0:T(8,128)} %param.12) | copy-start | bytes 49156
  6.1 35.7 %all-to-all-start = ((f32[16,256,128]{2,1,0:T(8,128)}), f32[16,256,128]{2,1,0:T(8,128)}, u32[]{:S(2)}, u32[]{:S(2)}) async-start(f32[16,256,128]{2,1,0:T(8,128)} %pad_maximum_fusion), calls=%async_computation | async-start | bytes 4194304 | tf_op jit(solution)/shard_map/all_to_all | solution.py:77
  42.8 30.8 %all-to-all-start.1 = ((f32[16,64,256]{2,1,0:T(8,128)}), f32[16,64,256]{2,1,0:T(8,128)S(1)}, u32[]{:S(2)}, u32[]{:S(2)}) async-start(f32[16,64,256]{2,1,0:T(8,128)} %stack.4), calls=%async_computation.1 | async-start | bytes 2097152 | tf_op jit(solution)/shard_map/all_to_all | solution.py:64
  48.5 7.1 %collective-permute-start.2 = (f32[256,128]{1,0:T(8,128)S(1)}, f32[256,128]{1,0:T(8,128)S(1)}, u32[]{:S(2)}, u32[]{:S(2)}) collective-permute-start(f32[256,128]{1,0:T(8,128)S(1)} %reduce_sum.73), channel_id=1, source_target_pairs={{0,3},{1,2},{2,1},{3,0},{4,7},{5,6},{6,5},{7,4},{8,11},{9,10},{10,... | collective-permute-start | bytes 393224 | tf_op jit(solution)/shard_map/ppermute | solution.py:39
  52.9 9.7 %collective-permute-start.1 = (f32[256,128]{1,0:T(8,128)S(1)}, f32[256,128]{1,0:T(8,128)S(1)}, u32[]{:S(2)}, u32[]{:S(2)}) collective-permute-start(f32[256,128]{1,0:T(8,128)S(1)} %reduce_sum.73), channel_id=1, source_target_pairs={{0,2},{1,3},{2,0},{3,1},{4,6},{5,7},{6,4},{7,5},{8,10},{9,11},{10,... | collective-permute-start | bytes 393224 | tf_op jit(solution)/shard_map/ppermute | solution.py:39
  52.9 9.7 %collective-permute-start = (f32[256,128]{1,0:T(8,128)S(1)}, f32[256,128]{1,0:T(8,128)S(1)}, u32[]{:S(2)}, u32[]{:S(2)}) collective-permute-start(f32[256,128]{1,0:T(8,128)S(1)} %reduce_sum.73), channel_id=1, source_target_pairs={{0,1},{1,0},{2,3},{3,2},{4,5},{5,4},{6,7},{7,6},{8,9},{9,8},{10,11... | collective-permute-start | bytes 393224 | tf_op jit(solution)/shard_map/ppermute | solution.py:39
  62.7 2.8 %collective-permute-start.3 = (f32[128,128]{1,0:T(8,128)S(1)}, f32[128,128]{1,0:T(8,128)S(1)}, u32[]{:S(2)}, u32[]{:S(2)}) collective-permute-start(f32[128,128]{1,0:T(8,128)S(1)} %slice.47), channel_id=1, source_target_pairs={{0,4},{4,0},{8,12},{12,8},{1,5},{5,1},{9,13},{13,9},{2,6},{6,2},{1... | collective-permute-start | bytes 196616 | tf_op jit(solution)/shard_map/ppermute | solution.py:39
  65.5 8.1 %collective-permute-start.4 = (f32[128,128]{1,0:T(8,128)S(1)}, f32[128,128]{1,0:T(8,128)S(1)}, u32[]{:S(2)}, u32[]{:S(2)}) collective-permute-start(f32[128,128]{1,0:T(8,128)S(1)} %get-tuple-element.18), channel_id=1, source_target_pairs={{0,8},{4,12},{8,0},{12,4},{1,9},{5,13},{9,1},{13,5},{2,10},{6,14},... | collective-permute-start | bytes 196616 | tf_op jit(solution)/shard_map/ppermute | solution.py:39
  73.6 1.6 %copy-start.1 = (f32[16,64,256]{2,1,0:T(8,128)}, f32[16,64,256]{2,1,0:T(8,128)S(1)}, u32[]{:S(2)}) copy-start(f32[16,64,256]{2,1,0:T(8,128)S(1)} %all-to-all-done.1) | copy-start | bytes 3145732
  75.3 6.9 %copy-start.6 = (s32[16]{0:T(128)S(1)}, s32[16]{0:T(128)}, u32[]{:S(2)}) copy-start(s32[16]{0:T(128)} %param.11) | copy-start | bytes 196
  75.3 33.4 %all-to-all-start.2 = ((f32[16,256,128]{2,1,0:T(8,128)}), f32[16,256,128]{2,1,0:T(8,128)}, u32[]{:S(2)}, u32[]{:S(2)}) async-start(f32[16,256,128]{2,1,0:T(8,128)} %broadcast_in_dim.33), calls=%async_computation.2 | async-start | bytes 4194304 | tf_op jit(solution)/shard_map/all_to_all | solution.py:84
  110.4 1.0 copy-start.2
